TPU v7x, 32 devices: a whole 2x2x4 slice. The times are simulated.
32 devices in a mesh: lon: 16 (over z, y, x), lat: 2 (over core).
Axes of the slice: x: 2, y: 2, z: 4, core: 2. Of those that a mesh axis runs over, the one named last changes fastest.
Arguments:
- sketch: float32 [64, 256, 512], P(None, 'lon', 'lat'), may hold values from -6 to 6
- probe_bits: int32 [2, 256, 512], P(None, 'lon', 'lat'), may hold values from 0 to 65535
- ocean: int32 [256, 512], P('lon', 'lat'), may hold values 0 or 1
- east_cond: float32 [256, 512], P('lon', 'lat'), may hold values from 0.2 to 2
- north_cond: float32 [256, 512], P('lon', 'lat'), may hold values from 0.1 to 1
- kappa_sq: float32 [256, 512], P('lon', 'lat'), may hold values from 0.05 to 0.5
- inv_area: float32 [256, 512], P('lon', 'lat'), may hold values from 0.05 to 0.2
Outputs:
- image_out: float32 [64, 256, 512], P(None, 'lon', 'lat')
- gram_out: float32 [96, 96], replicated
Inputs may be any that keep to these rules, and one draw needn't show every extreme that they name: `probe_bits`: each word holds 16 independent sign bits, bit b of word w giving probe column 16 w + b.
All inputs are finite; a program needn't handle non-finite values. No bound on the sum of `ocean` on one device may be relied on, other than what follows from the above.
Results may differ from a plain program's by a relative error of at most 0.00015.
Values sent between devices are 32-bit elements; how exact they have to be, the bound alone decides.
No kernel may reach another device: no remote copies, remote signals or barrier semaphores. Data moves between devices by JAX's collectives and lax.ppermute only.
A program may use at most 64 MiB of HBM per device.

v0:
```python
import jax
import jax.numpy as jnp
from jax import lax
from jax.sharding import PartitionSpec as P


def padded_2(cells, sides, width, closed):
    for axis, dim in sides:
        count = lax.axis_size(axis)
        ends = count if closed else count - 1
        head = lax.slice_in_dim(cells, 0, width, axis=dim)
        tail = lax.slice_in_dim(cells, cells.shape[dim] - width, cells.shape[dim], axis=dim)
        cells = jnp.concatenate(
            [
                lax.ppermute(tail, axis, [(i, (i + 1) % count) for i in range(ends)]),
                cells,
                lax.ppermute(head, axis, [((i + 1) % count, i) for i in range(ends)]),
            ],
            axis=dim,
        )
    return cells


def sign_columns(probe_bits):
    shifts = jnp.arange(16, dtype=jnp.int32)
    picked = jnp.right_shift(probe_bits[:, None], shifts[None, :, None, None])
    flipped = jnp.bitwise_and(picked, 1)
    return (1 - 2 * flipped).astype(jnp.float32).reshape((-1,) + probe_bits.shape[1:])


def operate(padded, weights):
    middle = padded[:, 1:-1, 1:-1]
    return weights[0] * (
        weights[1] * middle
        - weights[2] * padded[:, 2:, 1:-1]
        - weights[3] * padded[:, :-2, 1:-1]
        - weights[4] * padded[:, 1:-1, 2:]
        - weights[5] * padded[:, 1:-1, :-2]
    )


def extend(field_in, thickness):
    wider = padded_2(field_in, (("lon", 1),), thickness, True)
    return padded_2(wider, (("lat", 2),), thickness, False)


def pair_gram(left, right):
    left_flat = left.reshape(left.shape[0], -1)
    right_flat = right.reshape(right.shape[0], -1)
    return jnp.einsum("ac,bc->ab", left_flat, right_flat, precision=lax.Precision.HIGHEST)


def local(sketch, probe_bits, ocean, east_cond, north_cond, kappa_sq, inv_area):
    lon_count, lat_count = ocean.shape
    sea_mask = ocean.astype(jnp.float32)
    stacked = jnp.stack([sea_mask, east_cond, north_cond, kappa_sq, inv_area])
    widened = padded_2(stacked, (("lon", 1),), 2, True)
    widened = padded_2(widened, (("lat", 2),), 2, False)
    sea_wide = widened[0]
    east_wide = widened[1]
    north_wide = widened[2]
    kappa_wide = widened[3]
    area_wide = widened[4]
    east_edges = east_wide[:-1] * sea_wide[:-1] * sea_wide[1:]
    north_edges = north_wide[:, :-1] * sea_wide[:, :-1] * sea_wide[:, 1:]
    offset = 2 - 0
    span_lon = lon_count + 2 * 0
    span_lat = lat_count + 2 * 0

    def window(array, shift_lon, shift_lat):
        return array[
            offset + shift_lon : offset + shift_lon + span_lon,
            offset + shift_lat : offset + shift_lat + span_lat,
        ]

    east_weight = window(east_edges, 0, 0)
    west_weight = window(east_edges, -1, 0)
    north_weight = window(north_edges, 0, 0)
    south_weight = window(north_edges, 0, -1)
    center_term = window(kappa_wide, 0, 0) + east_weight + west_weight + north_weight + south_weight
    interior = (
        window(sea_wide, 0, 0),
        center_term,
        east_weight,
        west_weight,
        north_weight,
        south_weight,
        window(area_wide, 0, 0),
    )
    sketch_masked = sketch * sea_mask
    columns = jnp.concatenate([sketch_masked, sign_columns(probe_bits) * sea_mask], axis=0)
    sketch_count = sketch.shape[0]
    thickness = 1
    columns_wide = extend(columns, thickness)
    first_pass = operate(columns_wide, interior)
    scaled = first_pass * interior[6]
    second = operate(extend(scaled[:sketch_count], 1), interior)
    local_gram = pair_gram(first_pass, scaled)
    summed = lax.psum(local_gram, ("lon", "lat"))
    cell_total = lax.axis_size("lon") * lon_count * lax.axis_size("lat") * lat_count
    return (second, summed / cell_total)


def solution(mesh):
    in_specs = (
        P(None, "lon", "lat"),
        P(None, "lon", "lat"),
        P("lon", "lat"),
        P("lon", "lat"),
        P("lon", "lat"),
        P("lon", "lat"),
        P("lon", "lat"),
    )
    out_specs = (P(None, "lon", "lat"), P())
    return jax.shard_map(local, mesh=mesh, in_specs=in_specs, out_specs=out_specs, check_vma=False)
```

profile of v0, /device:TPU:13, one launch (start us, length us, event | category | flops | bytes accessed | tf_op | source)
XLA Modules:
  0.0 94.8 jit_solution(9568899763508457570)
XLA Ops:
  0.6 0.7 bitcast_dynamic-update-slice_fusion.4
  4.3 1.3 %collective-permute-start = (f32[5,2,256]{2,1,0:T(2,128)S(1)}, f32[5,2,256]{2,1,0:T(2,128)S(1)}, u32[]{:S(2)}, u32[]{:S(2)}) collective-permute-start(f32[5,2,256]{2,1,0:T(2,128)S(1)} %get-tuple-element.20), channel_id=1, source_target_pairs={{0,2},{2,4},{4,6},{6,8},{8,10},{10,12},{12,14},{14,16},{16,18},{18... | collective-permute-start | bytes 30728 | tf_op jit(solution)/shard_map/ppermute | solution.py:15
  5.5 1.2 %collective-permute-start.1 = (f32[5,2,256]{2,1,0:T(2,128)S(1)}, f32[5,2,256]{2,1,0:T(2,128)S(1)}, u32[]{:S(2)}, u32[]{:S(2)}) collective-permute-start(f32[5,2,256]{2,1,0:T(2,128)S(1)} %get-tuple-element.21), channel_id=1, source_target_pairs={{2,0},{4,2},{6,4},{8,6},{10,8},{12,10},{14,12},{16,14},{18,16},{20... | collective-permute-start | bytes 30728 | tf_op jit(solution)/shard_map/ppermute | solution.py:17
  7.4 1.8 %copy_multiply_fusion = f32[64,16,256]{2,0,1:T(8,128)S(1)} fusion(f32[64,16,256]{2,1,0:T(8,128)} %param.7, f32[16,256]{1,0:T(8,128)S(1)} %convert_element_type.7), kind=kLoop, calls=%fused_computation.47 | loop fusion | flops 262144 | bytes 2113536 | tf_op jit(solution)/shard_map/mul | solution.py:90
  9.7 1.3 %collective-permute-start.2 = (f32[5,20,2]{2,1,0:T(8,128)S(1)}, f32[5,20,2]{2,1,0:T(8,128)S(1)}, u32[]{:S(2)}, u32[]{:S(2)}) collective-permute-start(f32[5,20,2]{2,1,0:T(8,128)S(1)} %get-tuple-element.18), channel_id=1, source_target_pairs={{0,1},{2,3},{4,5},{6,7},{8,9},{10,11},{12,13},{14,15},{16,17},{18,... | collective-permute-start | bytes 2408 | tf_op jit(solution)/shard_map/ppermute | solution.py:15
  11.0 3.1 %collective-permute-start.3 = (f32[5,20,2]{2,1,0:T(8,128)S(1)}, f32[5,20,2]{2,1,0:T(8,128)S(1)}, u32[]{:S(2)}, u32[]{:S(2)}) collective-permute-start(f32[5,20,2]{2,1,0:T(8,128)S(1)} %get-tuple-element.19), channel_id=1, source_target_pairs={{1,0},{3,2},{5,4},{7,6},{9,8},{11,10},{13,12},{15,14},{17,16},{19,... | collective-permute-start | bytes 2408 | tf_op jit(solution)/shard_map/ppermute | solution.py:17
  14.1 2.4 %collective-permute-start.5 = (f32[96,1,256]{2,0,1:T(8,128)S(1)}, f32[96,1,256]{2,0,1:T(8,128)S(1)}, u32[]{:S(2)}, u32[]{:S(2)}) collective-permute-start(f32[96,1,256]{2,0,1:T(8,128)S(1)} %get-tuple-element.10), channel_id=1, source_target_pairs={{0,2},{2,4},{4,6},{6,8},{8,10},{10,12},{12,14},{14,16},{16,18},{18... | collective-permute-start | bytes 294920 | tf_op jit(solution)/shard_map/ppermute | solution.py:15
  18.7 0.9 collective-permute-done.5
  19.6 3.1 %collective-permute-done.4 = f32[96,1,256]{2,0,1:T(8,128)S(1)} collective-permute-done((f32[96,1,256]{2,0,1:T(8,128)S(1)}, f32[96,1,256]{2,0,1:T(8,128)S(1)}, u32[]{:S(2)}, u32[]{:S(2)}) %collective-permute-start.4) | collective-permute-done | bytes 98336 | tf_op jit(solution)/shard_map/ppermute | solution.py:17
  23.3 1.0 %copy.13 = f32[96,18,1]{0,1,2:T(8,128)} copy(f32[96,18,1]{2,0,1:T(8,128)S(1)} %get-tuple-element.6) | data formatting | bytes 13824 | tf_op jit(solution)/shard_map/slice | solution.py:11
  24.7 1.3 %collective-permute-start.7 = (f32[96,18,1]{0,1,2:T(8,128)S(1)}, f32[96,18,1]{0,1,2:T(8,128)}, u32[]{:S(2)}, u32[]{:S(2)}) collective-permute-start(f32[96,18,1]{0,1,2:T(8,128)S(1)} %copy.15), channel_id=1, source_target_pairs={{0,1},{2,3},{4,5},{6,7},{8,9},{10,11},{12,13},{14,15},{16,17},{18,... | collective-permute-start | bytes 20744 | tf_op jit(solution)/shard_map/ppermute | solution.py:15
  26.0 3.6 %collective-permute-start.6 = (f32[96,18,1]{0,1,2:T(8,128)}, f32[96,18,1]{0,1,2:T(8,128)S(1)}, u32[]{:S(2)}, u32[]{:S(2)}) collective-permute-start(f32[96,18,1]{0,1,2:T(8,128)} %copy.13), channel_id=1, source_target_pairs={{1,0},{3,2},{5,4},{7,6},{9,8},{11,10},{13,12},{15,14},{17,16},{19,... | collective-permute-start | bytes 20744 | tf_op jit(solution)/shard_map/ppermute | solution.py:17
  29.6 1.6 %fusion.29 = (f32[16,256]{1,0:T(8,128)S(1)}, f32[16,256]{1,0:T(8,128)}, f32[16,256]{1,0:T(8,128)}, f32[16,256]{1,0:T(8,128)}, f32[16,256]{1,0:T(8,128)}) fusion(f32[20,260]{1,0:T(8,128)} %get-tuple-element.14, f32[20,259]{1,0:T(8,128)} %slice_multiply_fusion, f32[19,260]{1,0:T(8,128)} %fusion.26), kind=kLoop, calls=%fused_computation.72 | loop fusion | flops 16384 | bytes 163840 | tf_op jit(solution)/shard_map/add | solution.py:80
  31.8 1.4 %slice.195 = f32[16,256]{1,0:T(8,128)} slice(f32[20,260]{1,0:T(8,128)} %get-tuple-element.15), slice={[2:18], [2:258]} | slice | bytes 32768 | tf_op jit(solution)/shard_map/slice | solution.py:71
  33.6 1.0 %copy.16 = f32[96,18,1]{2,0,1:T(8,128)S(1)} copy(f32[96,18,1]{0,1,2:T(8,128)} %collective-permute-done.7) | data formatting | bytes 13824 | tf_op jit(solution)/shard_map/ppermute | solution.py:15
  34.7 3.8 %broadcast_multiply_fusion = (f32[96,16,256]{2,0,1:T(8,128)S(1)}, f32[96,16,256]{2,0,1:T(8,128)S(1)}) fusion(f32[16,256]{1,0:T(8,128)} %slice.195, f32[96,1,256]{2,0,1:T(8,128)S(1)} %copy-done.1, f32[32,16,256]{2,0,1:T(8,128)S(1)} %fusion.23, f32[64,16,256]{2,0,1:T(8,128)S(1)} %copy_multiply_fusion, f32[96,1,256]{2,0,1:T(8,128)S(1)} %collective-permute-done.5, ...), kind=kLoop, calls=%fused_computation.48 | loop fusion | flops 9437184 | bytes 5043712 | tf_op jit(solution)/shard_map/mul | solution.py:96
  38.5 1.4 %collective-permute-start.9 = (f32[64,1,256]{2,0,1:T(8,128)S(1)}, f32[64,1,256]{2,0,1:T(8,128)S(1)}, u32[]{:S(2)}, u32[]{:S(2)}) collective-permute-start(f32[64,1,256]{2,0,1:T(8,128)S(1)} %get-tuple-element.8), channel_id=1, source_target_pairs={{0,2},{2,4},{4,6},{6,8},{8,10},{10,12},{12,14},{14,16},{16,18},{18... | collective-permute-start | bytes 196616 | tf_op jit(solution)/shard_map/ppermute | solution.py:15
  39.9 1.1 %collective-permute-start.8 = (f32[64,1,256]{2,0,1:T(8,128)S(1)}, f32[64,1,256]{2,0,1:T(8,128)S(1)}, u32[]{:S(2)}, u32[]{:S(2)}) collective-permute-start(f32[64,1,256]{2,0,1:T(8,128)S(1)} %get-tuple-element.9), channel_id=1, source_target_pairs={{2,0},{4,2},{6,4},{8,6},{10,8},{12,10},{14,12},{16,14},{18,16},{20... | collective-permute-start | bytes 196616 | tf_op jit(solution)/shard_map/ppermute | solution.py:17
  40.9 1.4 %convolution_bitcast_fusion = f32[96,96]{1,0:T(8,128)S(1)} fusion(f32[96,16,256]{2,0,1:T(8,128)S(1)} %get-tuple-element.5, f32[16,256]{1,0:T(8,128)S(1)} %copy-done.7), kind=kOutput, calls=%fused_computation.29 | convolution fusion | flops 453378048 | bytes 1626112 | tf_op jit(solution)/shard_map/ac,bc->ab/dot_general | solution.py:50
  42.4 42.2 %psum.7 = f32[96,96]{1,0:T(8,128)S(1)} all-reduce(f32[96,96]{1,0:T(8,128)S(1)} %convolution_bitcast_fusion), channel_id=1, replica_groups=mesh['lon'=16,'lat'=2] {'lon','lat'}, use_global_device_ids=true, to_apply=%region_0.0 | all-reduce | flops 9216 | bytes 73728 | tf_op jit(solution)/shard_map/psum | solution.py:99
  85.6 1.3 %collective-permute-start.11 = (f32[64,18,1]{0,1,2:T(8,128)S(1)}, f32[64,18,1]{0,1,2:T(8,128)S(1)}, u32[]{:S(2)}, u32[]{:S(2)}) collective-permute-start(f32[64,18,1]{0,1,2:T(8,128)S(1)} %copy.19), channel_id=1, source_target_pairs={{0,1},{2,3},{4,5},{6,7},{8,9},{10,11},{12,13},{14,15},{16,17},{18,... | collective-permute-start | bytes 13832 | tf_op jit(solution)/shard_map/ppermute | solution.py:15
  87.0 4.0 %collective-permute-start.10 = (f32[64,18,1]{0,1,2:T(8,128)S(1)}, f32[64,18,1]{0,1,2:T(8,128)S(1)}, u32[]{:S(2)}, u32[]{:S(2)}) collective-permute-start(f32[64,18,1]{0,1,2:T(8,128)S(1)} %copy.17), channel_id=1, source_target_pairs={{1,0},{3,2},{5,4},{7,6},{9,8},{11,10},{13,12},{15,14},{17,16},{19,... | collective-permute-start | bytes 13832 | tf_op jit(solution)/shard_map/ppermute | solution.py:17
  92.4 0.8 fusion.12
  93.2 1.6 %copy.21 = f32[64,16,256]{2,1,0:T(8,128)} copy(f32[64,16,256]{2,0,1:T(8,128)S(1)} %fusion.12) | data formatting | bytes 2097152
  (60 shorter events, 10.5 us)
Async XLA Ops:
  0.6 8.7 %copy-start.8 = (s32[2,16,256]{2,1,0:T(8,128)S(1)}, s32[2,16,256]{2,1,0:T(8,128)}, u32[]{:S(2)}) copy-start(s32[2,16,256]{2,1,0:T(8,128)} %param.8) | copy-start | bytes 98308
  4.3 5.3 %collective-permute-start = (f32[5,2,256]{2,1,0:T(2,128)S(1)}, f32[5,2,256]{2,1,0:T(2,128)S(1)}, u32[]{:S(2)}, u32[]{:S(2)}) collective-permute-start(f32[5,2,256]{2,1,0:T(2,128)S(1)} %get-tuple-element.20), channel_id=1, source_target_pairs={{0,2},{2,4},{4,6},{6,8},{8,10},{10,12},{12,14},{14,16},{16,18},{18... | collective-permute-start | bytes 30728 | tf_op jit(solution)/shard_map/ppermute | solution.py:15
  5.5 4.0 %collective-permute-start.1 = (f32[5,2,256]{2,1,0:T(2,128)S(1)}, f32[5,2,256]{2,1,0:T(2,128)S(1)}, u32[]{:S(2)}, u32[]{:S(2)}) collective-permute-start(f32[5,2,256]{2,1,0:T(2,128)S(1)} %get-tuple-element.21), channel_id=1, source_target_pairs={{2,0},{4,2},{6,4},{8,6},{10,8},{12,10},{14,12},{16,14},{18,16},{20... | collective-permute-start | bytes 30728 | tf_op jit(solution)/shard_map/ppermute | solution.py:17
  9.7 6.9 %collective-permute-start.2 = (f32[5,20,2]{2,1,0:T(8,128)S(1)}, f32[5,20,2]{2,1,0:T(8,128)S(1)}, u32[]{:S(2)}, u32[]{:S(2)}) collective-permute-start(f32[5,20,2]{2,1,0:T(8,128)S(1)} %get-tuple-element.18), channel_id=1, source_target_pairs={{0,1},{2,3},{4,5},{6,7},{8,9},{10,11},{12,13},{14,15},{16,17},{18,... | collective-permute-start | bytes 2408 | tf_op jit(solution)/shard_map/ppermute | solution.py:15
  11.0 5.6 %collective-permute-start.3 = (f32[5,20,2]{2,1,0:T(8,128)S(1)}, f32[5,20,2]{2,1,0:T(8,128)S(1)}, u32[]{:S(2)}, u32[]{:S(2)}) collective-permute-start(f32[5,20,2]{2,1,0:T(8,128)S(1)} %get-tuple-element.19), channel_id=1, source_target_pairs={{1,0},{3,2},{5,4},{7,6},{9,8},{11,10},{13,12},{15,14},{17,16},{19,... | collective-permute-start | bytes 2408 | tf_op jit(solution)/shard_map/ppermute | solution.py:17
  14.1 5.5 %collective-permute-start.5 = (f32[96,1,256]{2,0,1:T(8,128)S(1)}, f32[96,1,256]{2,0,1:T(8,128)S(1)}, u32[]{:S(2)}, u32[]{:S(2)}) collective-permute-start(f32[96,1,256]{2,0,1:T(8,128)S(1)} %get-tuple-element.10), channel_id=1, source_target_pairs={{0,2},{2,4},{4,6},{6,8},{8,10},{10,12},{12,14},{14,16},{16,18},{18... | collective-permute-start | bytes 294920 | tf_op jit(solution)/shard_map/ppermute | solution.py:15
  16.5 6.1 %collective-permute-start.4 = (f32[96,1,256]{2,0,1:T(8,128)S(1)}, f32[96,1,256]{2,0,1:T(8,128)S(1)}, u32[]{:S(2)}, u32[]{:S(2)}) collective-permute-start(f32[96,1,256]{2,0,1:T(8,128)S(1)} %get-tuple-element.11), channel_id=1, source_target_pairs={{2,0},{4,2},{6,4},{8,6},{10,8},{12,10},{14,12},{16,14},{18,16},{20... | collective-permute-start | bytes 294920 | tf_op jit(solution)/shard_map/ppermute | solution.py:17
  22.7 0.6 copy-start
  24.3 10.4 %copy-start.1 = (f32[96,1,256]{2,0,1:T(8,128)S(1)}, f32[96,1,256]{2,0,1:T(8,128)}, u32[]{:S(2)}) copy-start(f32[96,1,256]{2,0,1:T(8,128)} %copy-done) | copy-start | bytes 294916
  24.7 9.0 %collective-permute-start.7 = (f32[96,18,1]{0,1,2:T(8,128)S(1)}, f32[96,18,1]{0,1,2:T(8,128)}, u32[]{:S(2)}, u32[]{:S(2)}) collective-permute-start(f32[96,18,1]{0,1,2:T(8,128)S(1)} %copy.15), channel_id=1, source_target_pairs={{0,1},{2,3},{4,5},{6,7},{8,9},{10,11},{12,13},{14,15},{16,17},{18,... | collective-permute-start | bytes 20744 | tf_op jit(solution)/shard_map/ppermute | solution.py:15
  26.0 7.3 %collective-permute-start.6 = (f32[96,18,1]{0,1,2:T(8,128)}, f32[96,18,1]{0,1,2:T(8,128)S(1)}, u32[]{:S(2)}, u32[]{:S(2)}) collective-permute-start(f32[96,18,1]{0,1,2:T(8,128)} %copy.13), channel_id=1, source_target_pairs={{1,0},{3,2},{5,4},{7,6},{9,8},{11,10},{13,12},{15,14},{17,16},{19,... | collective-permute-start | bytes 20744 | tf_op jit(solution)/shard_map/ppermute | solution.py:17
  34.7 6.2 %copy-start.7 = (f32[16,256]{1,0:T(8,128)S(1)}, f32[16,256]{1,0:T(8,128)}, u32[]{:S(2)}) copy-start(f32[16,256]{1,0:T(8,128)} %slice.195) | copy-start | bytes 49156
  38.5 46.2 %collective-permute-start.9 = (f32[64,1,256]{2,0,1:T(8,128)S(1)}, f32[64,1,256]{2,0,1:T(8,128)S(1)}, u32[]{:S(2)}, u32[]{:S(2)}) collective-permute-start(f32[64,1,256]{2,0,1:T(8,128)S(1)} %get-tuple-element.8), channel_id=1, source_target_pairs={{0,2},{2,4},{4,6},{6,8},{8,10},{10,12},{12,14},{14,16},{16,18},{18... | collective-permute-start | bytes 196616 | tf_op jit(solution)/shard_map/ppermute | solution.py:15
  39.9 44.8 %collective-permute-start.8 = (f32[64,1,256]{2,0,1:T(8,128)S(1)}, f32[64,1,256]{2,0,1:T(8,128)S(1)}, u32[]{:S(2)}, u32[]{:S(2)}) collective-permute-start(f32[64,1,256]{2,0,1:T(8,128)S(1)} %get-tuple-element.9), channel_id=1, source_target_pairs={{2,0},{4,2},{6,4},{8,6},{10,8},{12,10},{14,12},{16,14},{18,16},{20... | collective-permute-start | bytes 196616 | tf_op jit(solution)/shard_map/ppermute | solution.py:17
  85.0 7.3 %copy-start.2 = (f32[16,256]{1,0:T(8,128)S(1)}, f32[16,256]{1,0:T(8,128)}, u32[]{:S(2)}) copy-start(f32[16,256]{1,0:T(8,128)} %get-tuple-element.23) | copy-start | bytes 49156
  85.0 7.3 %copy-start.3 = (f32[16,256]{1,0:T(8,128)S(1)}, f32[16,256]{1,0:T(8,128)}, u32[]{:S(2)}) copy-start(f32[16,256]{1,0:T(8,128)} %get-tuple-element.24) | copy-start | bytes 49156
  85.0 7.3 %copy-start.4 = (f32[16,256]{1,0:T(8,128)S(1)}, f32[16,256]{1,0:T(8,128)}, u32[]{:S(2)}) copy-start(f32[16,256]{1,0:T(8,128)} %get-tuple-element.25) | copy-start | bytes 49156
  85.0 7.3 %copy-start.5 = (f32[16,256]{1,0:T(8,128)S(1)}, f32[16,256]{1,0:T(8,128)}, u32[]{:S(2)}) copy-start(f32[16,256]{1,0:T(8,128)} %get-tuple-element.26) | copy-start | bytes 49156
  85.1 7.3 %copy-start.6 = (f32[16,256]{1,0:T(8,128)S(1)}, f32[16,256]{1,0:T(8,128)}, u32[]{:S(2)}) copy-start(f32[16,256]{1,0:T(8,128)} %slice.174) | copy-start | bytes 49156
  85.6 6.4 %collective-permute-start.11 = (f32[64,18,1]{0,1,2:T(8,128)S(1)}, f32[64,18,1]{0,1,2:T(8,128)S(1)}, u32[]{:S(2)}, u32[]{:S(2)}) collective-permute-start(f32[64,18,1]{0,1,2:T(8,128)S(1)} %copy.19), channel_id=1, source_target_pairs={{0,1},{2,3},{4,5},{6,7},{8,9},{10,11},{12,13},{14,15},{16,17},{18,... | collective-permute-start | bytes 13832 | tf_op jit(solution)/shard_map/ppermute | solution.py:15
  87.0 4.9 %collective-permute-start.10 = (f32[64,18,1]{0,1,2:T(8,128)S(1)}, f32[64,18,1]{0,1,2:T(8,128)S(1)}, u32[]{:S(2)}, u32[]{:S(2)}) collective-permute-start(f32[64,18,1]{0,1,2:T(8,128)S(1)} %copy.17), channel_id=1, source_target_pairs={{1,0},{3,2},{5,4},{7,6},{9,8},{11,10},{13,12},{15,14},{17,16},{19,... | collective-permute-start | bytes 13832 | tf_op jit(solution)/shard_map/ppermute | solution.py:17
where the time goes:
time: 95.8 us; the launch traced here: 94.8 us
  blocking collectives  42.2 us (44%)
  starting transfers between devices  21.9 us (23%)
  local copies, waits for them, and re-layouts  12.1 us (13%)
  other arithmetic  11.9 us (12%)
  waiting for transfers between devices  4.22 us (4%)
  matrix products  1.45 us (2%)
  between operations  0.98 us (1%)
    psum x1, blocking collectives, local(): summed = lax.psum(local_gram, ('lon', 'lat'))  42.2 us
    ppermute x6, starting transfers between devices, padded_2(): lax.ppermute(head, axis, [((i + 1) % count, i) for i in range(ends)])  13 us
    ppermute x6, starting transfers between devices, padded_2(): lax.ppermute(tail, axis, [(i, (i + 1) % count) for i in range(ends)])  8.92 us
    unnamed x23, local copies, waits for them, and re-layouts  4.01 us
    mul x1, other arithmetic, local(): scaled = first_pass * interior[6]  3.76 us
    ppermute x6, waiting for transfers between devices, padded_2(): lax.ppermute(head, axis, [((i + 1) % count, i) for i in range(ends)])  3.28 us
    slice x2, local copies, waits for them, and re-layouts, window(): array[offset + shift_lon:offset + shift_lon + span_lon, offset + shift_la...  2.12 us
  transfers between devices with their start and end apart: 12, of which 3 were waited for; matrix products, arithmetic and copies ran while one was open for 12% of the time, Pallas kernels for 0%

commit v1 on v0

--- a/solution.py
+++ b/solution.py
@@ -96,7 +96,8 @@
     scaled = first_pass * interior[6]
     second = operate(extend(scaled[:sketch_count], 1), interior)
     local_gram = pair_gram(first_pass, scaled)
-    summed = lax.psum(local_gram, ("lon", "lat"))
+    block_next = lax.psum(local_gram, "lat")
+    summed = lax.psum(block_next, "lon")
     cell_total = lax.axis_size("lon") * lon_count * lax.axis_size("lat") * lat_count
     return (second, summed / cell_total)
 

time: 95.8 us -> 136 us (1.42)
  the two profiles are of different devices: /device:TPU:13 before, /device:TPU:0 now
where the time goes in v1:
time: 136 us; the launch traced here: 135 us
  blocking collectives  77.5 us (57%)
  starting transfers between devices  27.7 us (20%)
  local copies, waits for them, and re-layouts  12.7 us (9%)
  other arithmetic  11.9 us (9%)
  waiting for transfers between devices  2.5 us (2%)
  matrix products  1.45 us (1%)
    psum x1, blocking collectives, local(): summed = lax.psum(block_next, 'lon')  73.4 us
    ppermute x6, starting transfers between devices, padded_2(): lax.ppermute(head, axis, [((i + 1) % count, i) for i in range(ends)])  19.1 us
    ppermute x6, starting transfers between devices, padded_2(): lax.ppermute(tail, axis, [(i, (i + 1) % count) for i in range(ends)])  8.51 us
    unnamed x23, local copies, waits for them, and re-layouts  4.62 us
    psum x1, blocking collectives, local(): block_next = lax.psum(local_gram, 'lat')  4.14 us
    mul x1, other arithmetic, local(): scaled = first_pass * interior[6]  3.76 us
  transfers between devices with their start and end apart: 12, of which 2 were waited for; matrix products, arithmetic and copies ran while one was open for 7% of the time, Pallas kernels for 0%

profile of v1, /device:TPU:0, one launch (start us, length us, event | category | flops | bytes accessed | tf_op | source)
XLA Modules:
  0.0 134.7 jit_solution(13255393844321951061)
XLA Ops:
  0.6 0.7 bitcast_dynamic-update-slice_fusion.4
  4.3 3.0 %collective-permute-start = (f32[5,2,256]{2,1,0:T(2,128)S(1)}, f32[5,2,256]{2,1,0:T(2,128)S(1)}, u32[]{:S(2)}, u32[]{:S(2)}) collective-permute-start(f32[5,2,256]{2,1,0:T(2,128)S(1)} %get-tuple-element.20), channel_id=1, source_target_pairs={{0,2},{2,4},{4,6},{6,8},{8,10},{10,12},{12,14},{14,16},{16,18},{18... | collective-permute-start | bytes 30728 | tf_op jit(solution)/shard_map/ppermute | solution.py:15
  7.3 4.1 %collective-permute-start.1 = (f32[5,2,256]{2,1,0:T(2,128)S(1)}, f32[5,2,256]{2,1,0:T(2,128)S(1)}, u32[]{:S(2)}, u32[]{:S(2)}) collective-permute-start(f32[5,2,256]{2,1,0:T(2,128)S(1)} %get-tuple-element.21), channel_id=1, source_target_pairs={{2,0},{4,2},{6,4},{8,6},{10,8},{12,10},{14,12},{16,14},{18,16},{20... | collective-permute-start | bytes 30728 | tf_op jit(solution)/shard_map/ppermute | solution.py:17
  12.1 1.8 %copy_multiply_fusion = f32[64,16,256]{2,0,1:T(8,128)S(1)} fusion(f32[64,16,256]{2,1,0:T(8,128)} %param.7, f32[16,256]{1,0:T(8,128)S(1)} %convert_element_type.7), kind=kLoop, calls=%fused_computation.47 | loop fusion | flops 262144 | bytes 2113536 | tf_op jit(solution)/shard_map/mul | solution.py:90
  14.3 1.5 %collective-permute-start.2 = (f32[5,20,2]{2,1,0:T(8,128)S(1)}, f32[5,20,2]{2,1,0:T(8,128)S(1)}, u32[]{:S(2)}, u32[]{:S(2)}) collective-permute-start(f32[5,20,2]{2,1,0:T(8,128)S(1)} %get-tuple-element.18), channel_id=1, source_target_pairs={{0,1},{2,3},{4,5},{6,7},{8,9},{10,11},{12,13},{14,15},{16,17},{18,... | collective-permute-start | bytes 2408 | tf_op jit(solution)/shard_map/ppermute | solution.py:15
  15.8 1.3 collective-permute-start.3
  17.2 5.6 %collective-permute-start.4 = (f32[96,1,256]{2,0,1:T(8,128)S(1)}, f32[96,1,256]{2,0,1:T(8,128)S(1)}, u32[]{:S(2)}, u32[]{:S(2)}) collective-permute-start(f32[96,1,256]{2,0,1:T(8,128)S(1)} %get-tuple-element.11), channel_id=1, source_target_pairs={{2,0},{4,2},{6,4},{8,6},{10,8},{12,10},{14,12},{16,14},{18,16},{20... | collective-permute-start | bytes 294920 | tf_op jit(solution)/shard_map/ppermute | solution.py:17
  24.9 1.3 collective-permute-done.5
  26.9 1.0 copy.13
  28.3 2.6 %collective-permute-start.7 = (f32[96,18,1]{0,1,2:T(8,128)S(1)}, f32[96,18,1]{0,1,2:T(8,128)}, u32[]{:S(2)}, u32[]{:S(2)}) collective-permute-start(f32[96,18,1]{0,1,2:T(8,128)S(1)} %copy.15), channel_id=1, source_target_pairs={{0,1},{2,3},{4,5},{6,7},{8,9},{10,11},{12,13},{14,15},{16,17},{18,... | collective-permute-start | bytes 20744 | tf_op jit(solution)/shard_map/ppermute | solution.py:15
  30.9 1.3 collective-permute-start.6
  32.2 1.5 %fusion.29 = (f32[16,256]{1,0:T(8,128)S(1)}, f32[16,256]{1,0:T(8,128)}, f32[16,256]{1,0:T(8,128)}, f32[16,256]{1,0:T(8,128)}, f32[16,256]{1,0:T(8,128)}) fusion(f32[20,260]{1,0:T(8,128)} %get-tuple-element.14, f32[20,259]{1,0:T(8,128)} %slice_multiply_fusion, f32[19,260]{1,0:T(8,128)} %fusion.26), kind=kLoop, calls=%fused_computation.72 | loop fusion | flops 16384 | bytes 163840 | tf_op jit(solution)/shard_map/add | solution.py:80
  34.4 1.4 %slice.195 = f32[16,256]{1,0:T(8,128)} slice(f32[20,260]{1,0:T(8,128)} %get-tuple-element.15), slice={[2:18], [2:258]} | slice | bytes 32768 | tf_op jit(solution)/shard_map/slice | solution.py:71
  36.2 1.0 copy.16
  37.3 3.8 %broadcast_multiply_fusion = (f32[96,16,256]{2,0,1:T(8,128)S(1)}, f32[96,16,256]{2,0,1:T(8,128)S(1)}) fusion(f32[16,256]{1,0:T(8,128)} %slice.195, f32[96,1,256]{2,0,1:T(8,128)S(1)} %copy-done.1, f32[32,16,256]{2,0,1:T(8,128)S(1)} %fusion.23, f32[64,16,256]{2,0,1:T(8,128)S(1)} %copy_multiply_fusion, f32[96,1,256]{2,0,1:T(8,128)S(1)} %collective-permute-done.5, ...), kind=kLoop, calls=%fused_computation.48 | loop fusion | flops 9437184 | bytes 5043712 | tf_op jit(solution)/shard_map/mul | solution.py:96
  41.7 1.5 %convolution_bitcast_fusion = f32[96,96]{1,0:T(8,128)S(1)} fusion(f32[96,16,256]{2,0,1:T(8,128)S(1)} %get-tuple-element.5, f32[16,256]{1,0:T(8,128)S(1)} %copy-done.7), kind=kOutput, calls=%fused_computation.29 | convolution fusion | flops 453378048 | bytes 1626112 | tf_op jit(solution)/shard_map/ac,bc->ab/dot_general | solution.py:50
  43.3 5.6 %collective-permute-start.8 = (f32[64,1,256]{2,0,1:T(8,128)S(1)}, f32[64,1,256]{2,0,1:T(8,128)S(1)}, u32[]{:S(2)}, u32[]{:S(2)}) collective-permute-start(f32[64,1,256]{2,0,1:T(8,128)S(1)} %get-tuple-element.9), channel_id=1, source_target_pairs={{2,0},{4,2},{6,4},{8,6},{10,8},{12,10},{14,12},{16,14},{18,16},{20... | collective-permute-start | bytes 196616 | tf_op jit(solution)/shard_map/ppermute | solution.py:17
  48.9 4.1 %psum.14 = f32[96,96]{1,0:T(8,128)S(1)} all-reduce(f32[96,96]{1,0:T(8,128)S(1)} %convolution_bitcast_fusion), channel_id=1, replica_groups=mesh['lon'=16,'lat'=2] {'lat'}, use_global_device_ids=true, to_apply=%region_0.0 | all-reduce | flops 9216 | bytes 73728 | tf_op jit(solution)/shard_map/psum | solution.py:99
  53.0 73.4 %psum.15 = f32[96,96]{1,0:T(8,128)S(1)} all-reduce(f32[96,96]{1,0:T(8,128)S(1)} %psum.14), channel_id=1, replica_groups=mesh['lon'=16,'lat'=2] {'lon'}, use_global_device_ids=true, to_apply=%region_1.0 | all-reduce | flops 9216 | bytes 73728 | tf_op jit(solution)/shard_map/psum | solution.py:100
  127.4 1.3 collective-permute-start.11
  128.7 1.3 collective-permute-start.10
  130.6 1.1 collective-permute-done.10
  132.4 0.8 fusion.12
  133.2 1.6 %copy.21 = f32[64,16,256]{2,1,0:T(8,128)} copy(f32[64,16,256]{2,0,1:T(8,128)S(1)} %fusion.12) | data formatting | bytes 2097152
  (61 shorter events, 11.1 us)
Async XLA Ops:
  0.6 13.4 %copy-start.8 = (s32[2,16,256]{2,1,0:T(8,128)S(1)}, s32[2,16,256]{2,1,0:T(8,128)}, u32[]{:S(2)}) copy-start(s32[2,16,256]{2,1,0:T(8,128)} %param.8) | copy-start | bytes 98308
  4.3 9.9 %collective-permute-start = (f32[5,2,256]{2,1,0:T(2,128)S(1)}, f32[5,2,256]{2,1,0:T(2,128)S(1)}, u32[]{:S(2)}, u32[]{:S(2)}) collective-permute-start(f32[5,2,256]{2,1,0:T(2,128)S(1)} %get-tuple-element.20), channel_id=1, source_target_pairs={{0,2},{2,4},{4,6},{6,8},{8,10},{10,12},{12,14},{14,16},{16,18},{18... | collective-permute-start | bytes 30728 | tf_op jit(solution)/shard_map/ppermute | solution.py:15
  7.3 6.9 %collective-permute-start.1 = (f32[5,2,256]{2,1,0:T(2,128)S(1)}, f32[5,2,256]{2,1,0:T(2,128)S(1)}, u32[]{:S(2)}, u32[]{:S(2)}) collective-permute-start(f32[5,2,256]{2,1,0:T(2,128)S(1)} %get-tuple-element.21), channel_id=1, source_target_pairs={{2,0},{4,2},{6,4},{8,6},{10,8},{12,10},{14,12},{16,14},{18,16},{20... | collective-permute-start | bytes 30728 | tf_op jit(solution)/shard_map/ppermute | solution.py:17
  14.3 8.5 %collective-permute-start.2 = (f32[5,20,2]{2,1,0:T(8,128)S(1)}, f32[5,20,2]{2,1,0:T(8,128)S(1)}, u32[]{:S(2)}, u32[]{:S(2)}) collective-permute-start(f32[5,20,2]{2,1,0:T(8,128)S(1)} %get-tuple-element.18), channel_id=1, source_target_pairs={{0,1},{2,3},{4,5},{6,7},{8,9},{10,11},{12,13},{14,15},{16,17},{18,... | collective-permute-start | bytes 2408 | tf_op jit(solution)/shard_map/ppermute | solution.py:15
  15.8 7.0 %collective-permute-start.3 = (f32[5,20,2]{2,1,0:T(8,128)S(1)}, f32[5,20,2]{2,1,0:T(8,128)S(1)}, u32[]{:S(2)}, u32[]{:S(2)}) collective-permute-start(f32[5,20,2]{2,1,0:T(8,128)S(1)} %get-tuple-element.19), channel_id=1, source_target_pairs={{1,0},{3,2},{5,4},{7,6},{9,8},{11,10},{13,12},{15,14},{17,16},{19,... | collective-permute-start | bytes 2408 | tf_op jit(solution)/shard_map/ppermute | solution.py:17
  17.1 9.2 %collective-permute-start.5 = (f32[96,1,256]{2,0,1:T(8,128)S(1)}, f32[96,1,256]{2,0,1:T(8,128)S(1)}, u32[]{:S(2)}, u32[]{:S(2)}) collective-permute-start(f32[96,1,256]{2,0,1:T(8,128)S(1)} %get-tuple-element.10), channel_id=1, source_target_pairs={{0,2},{2,4},{4,6},{6,8},{8,10},{10,12},{12,14},{14,16},{16,18},{18... | collective-permute-start | bytes 294920 | tf_op jit(solution)/shard_map/ppermute | solution.py:15
  17.2 9.1 %collective-permute-start.4 = (f32[96,1,256]{2,0,1:T(8,128)S(1)}, f32[96,1,256]{2,0,1:T(8,128)S(1)}, u32[]{:S(2)}, u32[]{:S(2)}) collective-permute-start(f32[96,1,256]{2,0,1:T(8,128)S(1)} %get-tuple-element.11), channel_id=1, source_target_pairs={{2,0},{4,2},{6,4},{8,6},{10,8},{12,10},{14,12},{16,14},{18,16},{20... | collective-permute-start | bytes 294920 | tf_op jit(solution)/shard_map/ppermute | solution.py:17
  26.3 0.6 copy-start
  27.9 9.4 %copy-start.1 = (f32[96,1,256]{2,0,1:T(8,128)S(1)}, f32[96,1,256]{2,0,1:T(8,128)}, u32[]{:S(2)}) copy-start(f32[96,1,256]{2,0,1:T(8,128)} %copy-done) | copy-start | bytes 294916
  28.3 7.9 %collective-permute-start.7 = (f32[96,18,1]{0,1,2:T(8,128)S(1)}, f32[96,18,1]{0,1,2:T(8,128)}, u32[]{:S(2)}, u32[]{:S(2)}) collective-permute-start(f32[96,18,1]{0,1,2:T(8,128)S(1)} %copy.15), channel_id=1, source_target_pairs={{0,1},{2,3},{4,5},{6,7},{8,9},{10,11},{12,13},{14,15},{16,17},{18,... | collective-permute-start | bytes 20744 | tf_op jit(solution)/shard_map/ppermute | solution.py:15
  30.9 5.0 %collective-permute-start.6 = (f32[96,18,1]{0,1,2:T(8,128)}, f32[96,18,1]{0,1,2:T(8,128)S(1)}, u32[]{:S(2)}, u32[]{:S(2)}) collective-permute-start(f32[96,18,1]{0,1,2:T(8,128)} %copy.13), channel_id=1, source_target_pairs={{1,0},{3,2},{5,4},{7,6},{9,8},{11,10},{13,12},{15,14},{17,16},{19,... | collective-permute-start | bytes 20744 | tf_op jit(solution)/shard_map/ppermute | solution.py:17
  41.0 0.7 copy-start.7
  43.2 83.2 %collective-permute-start.9 = (f32[64,1,256]{2,0,1:T(8,128)S(1)}, f32[64,1,256]{2,0,1:T(8,128)S(1)}, u32[]{:S(2)}, u32[]{:S(2)}) collective-permute-start(f32[64,1,256]{2,0,1:T(8,128)S(1)} %get-tuple-element.8), channel_id=1, source_target_pairs={{0,2},{2,4},{4,6},{6,8},{8,10},{10,12},{12,14},{14,16},{16,18},{18... | collective-permute-start | bytes 196616 | tf_op jit(solution)/shard_map/ppermute | solution.py:15
  43.3 83.1 %collective-permute-start.8 = (f32[64,1,256]{2,0,1:T(8,128)S(1)}, f32[64,1,256]{2,0,1:T(8,128)S(1)}, u32[]{:S(2)}, u32[]{:S(2)}) collective-permute-start(f32[64,1,256]{2,0,1:T(8,128)S(1)} %get-tuple-element.9), channel_id=1, source_target_pairs={{2,0},{4,2},{6,4},{8,6},{10,8},{12,10},{14,12},{16,14},{18,16},{20... | collective-permute-start | bytes 196616 | tf_op jit(solution)/shard_map/ppermute | solution.py:17
  126.8 5.6 %copy-start.2 = (f32[16,256]{1,0:T(8,128)S(1)}, f32[16,256]{1,0:T(8,128)}, u32[]{:S(2)}) copy-start(f32[16,256]{1,0:T(8,128)} %get-tuple-element.23) | copy-start | bytes 49156
  126.8 5.6 %copy-start.3 = (f32[16,256]{1,0:T(8,128)S(1)}, f32[16,256]{1,0:T(8,128)}, u32[]{:S(2)}) copy-start(f32[16,256]{1,0:T(8,128)} %get-tuple-element.24) | copy-start | bytes 49156
  126.8 5.6 %copy-start.4 = (f32[16,256]{1,0:T(8,128)S(1)}, f32[16,256]{1,0:T(8,128)}, u32[]{:S(2)}) copy-start(f32[16,256]{1,0:T(8,128)} %get-tuple-element.25) | copy-start | bytes 49156
  126.8 5.6 %copy-start.5 = (f32[16,256]{1,0:T(8,128)S(1)}, f32[16,256]{1,0:T(8,128)}, u32[]{:S(2)}) copy-start(f32[16,256]{1,0:T(8,128)} %get-tuple-element.26) | copy-start | bytes 49156
  126.8 5.6 %copy-start.6 = (f32[16,256]{1,0:T(8,128)S(1)}, f32[16,256]{1,0:T(8,128)}, u32[]{:S(2)}) copy-start(f32[16,256]{1,0:T(8,128)} %slice.174) | copy-start | bytes 49156
  127.4 4.6 %collective-permute-start.11 = (f32[64,18,1]{0,1,2:T(8,128)S(1)}, f32[64,18,1]{0,1,2:T(8,128)S(1)}, u32[]{:S(2)}, u32[]{:S(2)}) collective-permute-start(f32[64,18,1]{0,1,2:T(8,128)S(1)} %copy.19), channel_id=1, source_target_pairs={{0,1},{2,3},{4,5},{6,7},{8,9},{10,11},{12,13},{14,15},{16,17},{18,... | collective-permute-start | bytes 13832 | tf_op jit(solution)/shard_map/ppermute | solution.py:15
  128.7 3.1 %collective-permute-start.10 = (f32[64,18,1]{0,1,2:T(8,128)S(1)}, f32[64,18,1]{0,1,2:T(8,128)S(1)}, u32[]{:S(2)}, u32[]{:S(2)}) collective-permute-start(f32[64,18,1]{0,1,2:T(8,128)S(1)} %copy.17), channel_id=1, source_target_pairs={{1,0},{3,2},{5,4},{7,6},{9,8},{11,10},{13,12},{15,14},{17,16},{19,... | collective-permute-start | bytes 13832 | tf_op jit(solution)/shard_map/ppermute | solution.py:17
